TPU v7x, 128 devices: a whole 4x4x4 slice. The times are simulated.
128 devices in a mesh: ep: 32 (over z, y, core), dp: 4 (over x).
Axes of the slice: x: 4, y: 4, z: 4, core: 2. Of those that a mesh axis runs over, the one named last changes fastest.
Arguments:
- tokens: bfloat16 [2048, 7168], P(('ep', 'dp')), may hold values from -6 to 6
- routes: int32 [2048, 8], P(('ep', 'dp')), may hold values from 0 to 31, all different within a row; in each aligned block of 16 rows (0 to 15, 16 to 31, ...) at most 8 rows name the same one
- route_logits: float32 [2048, 8], P(('ep', 'dp')), may hold values from -6 to 6
- gate_weight: bfloat16 [32, 7168, 2048], P('ep', None, 'dp'), may hold values from -0.0625 to 0.0625
- up_weight: bfloat16 [32, 7168, 2048], P('ep', None, 'dp'), may hold values from -0.0625 to 0.0625
- down_weight: bfloat16 [32, 2048, 7168], P('ep', 'dp'), may hold values from -0.125 to 0.125
Outputs:
- moe_output: bfloat16 [2048, 7168], P(('ep', 'dp'))
- expert_load: float32 [32], P('ep')
Inputs may be any that keep to these rules, and one draw needn't show every extreme that they name: `routes`: each row names 8 different experts. Within the rows of one device (aligned blocks of 16 rows) no expert is named more than 8 times, and in every draw some expert is named exactly 8 times there; every expert is named somewhere.
All inputs are finite; a program needn't handle non-finite values.
Results may differ from a plain program's by a relative error of at most 0.012.
Values may be sent and summed in bfloat16 or wider, within the bound.
No kernel may reach another device: no remote copies, remote signals or barrier semaphores. Data moves between devices by JAX's collectives and lax.ppermute only.
A program may use at most 128 MiB of HBM per device.

v0:
```python
import jax
import jax.numpy as jnp
from jax import lax
from jax.sharding import Mesh
from jax.sharding import PartitionSpec as P

EP = ("ep_0", "ep_1", "ep_2")
EP_DP = ("ep_0", "ep_1", "ep_2", "dp")
ROUTE_SCALE = 2.5
PRECISE = lax.Precision.HIGHEST


def split_up(x, dim, devices):
    before, after = (x.shape[:dim], x.shape[dim + 1 :])
    return jnp.moveaxis(x.reshape(*before, devices, -1, *after), dim, 0)


def laid_out(parts, dim):
    lengths = list(parts.shape[1:])
    lengths[dim] *= parts.shape[0]
    return jnp.moveaxis(parts, 0, dim).reshape(lengths)


def moved_by_axis(parts, axes, order):
    lengths = [lax.axis_size(a) for a in axes]
    parts = parts.reshape(*lengths, *parts.shape[1:])
    for k in order:
        parts = lax.all_to_all(parts, axes[k], split_axis=k, concat_axis=k, tiled=True)
    return parts.reshape(-1, *parts.shape[len(axes) :])


def core_and_chips(x, groups, order, split_dim, concat_dim):
    devices = lax.axis_size(groups[0]) * lax.axis_size(groups[1])
    parts = split_up(x, split_dim, devices)
    return laid_out(moved_by_axis(parts, groups, order), concat_dim)


def sum_at_owner(x, axis, dim):
    devices = lax.axis_size(axis)
    parts = lax.all_to_all(split_up(x, dim, devices), axis, 0, 0, tiled=True)
    return jnp.sum(parts, axis=0)


def sent_to_all(x, axis):
    copies = jnp.broadcast_to(x, (lax.axis_size(axis), *x.shape))
    return lax.all_to_all(copies, axis, split_axis=0, concat_axis=0, tiled=True)


def over_copies(x, axis):
    return sent_to_all(x, axis).sum(axis=0)


def assignment_slots(flat_routes, experts):
    labels = jnp.arange(experts, dtype=jnp.int32)
    onehot = (flat_routes[:, :, None] == labels[None, None, :]).astype(jnp.int32)
    before = jnp.cumsum(onehot, axis=1) - onehot
    return (jnp.sum(before * onehot, axis=2), jnp.sum(onehot, axis=1))


def pack(members, flat_routes, slot_ids, experts, capacity, top_k):
    blocks, per_block = flat_routes.shape
    tok_dev = per_block // top_k
    member = jnp.arange(blocks, dtype=jnp.int32)[:, None]
    target = ((member * experts + flat_routes) * capacity + slot_ids).reshape(-1)
    source = (member * tok_dev + jnp.arange(per_block, dtype=jnp.int32)[None, :] // top_k).reshape(
        -1
    )
    placing = (
        jnp.arange(blocks * experts * capacity, dtype=jnp.int32)[:, None] == target[None, :]
    ).astype(jnp.bfloat16)
    owners = (source[:, None] == jnp.arange(blocks * tok_dev, dtype=jnp.int32)[None, :]).astype(
        jnp.bfloat16
    )
    picker = jnp.dot(placing, owners, preferred_element_type=jnp.float32).astype(jnp.bfloat16)
    filled = jnp.dot(picker, members, preferred_element_type=jnp.float32).astype(jnp.bfloat16)
    return filled.reshape(blocks, experts, capacity, members.shape[1])


def expert_rows(row_block, gate_w, up_w, down_w):
    gate_act = jnp.dot(row_block, gate_w, preferred_element_type=jnp.float32)
    up_act = jnp.dot(row_block, up_w, preferred_element_type=jnp.float32)
    hidden = (jax.nn.silu(gate_act) * up_act).astype(jnp.bfloat16)
    return jnp.dot(hidden, down_w, preferred_element_type=jnp.float32)


def on_device(tokens, routes, route_logits, gate_weight, up_weight, down_weight):
    tok_dev, top_k = routes.shape
    model_width = tokens.shape[1]
    experts = lax.axis_size(EP)
    groups = lax.axis_size("dp")
    capacity = min(tok_dev // 2, 2 * tok_dev * top_k // experts)
    per_block = tok_dev * top_k
    gate_w = gate_weight[0]
    up_w = up_weight[0]
    down_w = down_weight[0]
    own_flat = routes.reshape(1, per_block)
    own_slots, own_counts = assignment_slots(own_flat, experts)
    buffer = pack(tokens, own_flat, own_slots, experts, capacity, top_k)
    received = core_and_chips(buffer, (("ep_0", "ep_1"), "ep_2"), (1, 0), 1, 1)
    partial_value = expert_rows(
        lax.all_gather(received.reshape(-1, model_width), "dp", axis=0, tiled=True),
        gate_w,
        up_w,
        down_w,
    )
    shares = lax.psum_scatter(
        partial_value.astype(jnp.bfloat16), "dp", scatter_dimension=0, tiled=True
    ).astype(jnp.float32)
    returned = lax.all_to_all(
        shares.reshape(experts, capacity, model_width).astype(jnp.bfloat16),
        EP,
        split_axis=0,
        concat_axis=0,
        tiled=True,
    ).astype(jnp.float32)
    affinity = jax.nn.sigmoid(route_logits)
    weights = (ROUTE_SCALE * affinity / jnp.sum(affinity, axis=1, keepdims=True)).reshape(-1)
    own_target = own_flat[0] * capacity + own_slots[0]
    spread = jnp.where(
        own_target[:, None] == jnp.arange(experts * capacity, dtype=jnp.int32)[None, :],
        weights[:, None],
        0.0,
    )
    owners = (
        jnp.arange(tok_dev, dtype=jnp.int32)[:, None]
        == jnp.arange(per_block, dtype=jnp.int32)[None, :] // top_k
    ).astype(jnp.float32)
    combine = jnp.dot(owners, spread, precision=PRECISE)
    moe_output = jnp.dot(
        combine, returned.reshape(experts * capacity, model_width), precision=PRECISE
    ).astype(jnp.bfloat16)
    local_counts = own_counts[0].astype(jnp.float32)
    group_count = sum_at_owner(local_counts, EP, 0)
    expert_count = over_copies(group_count, "dp")
    mean_count = float(tok_dev * groups * top_k)
    expert_load = expert_count / mean_count
    return (moe_output, expert_load)


def solution(mesh):
    finer = Mesh(mesh.devices.reshape(4, 4, 2, mesh.shape["dp"]), ("ep_0", "ep_1", "ep_2", "dp"))
    in_specs = (
        P(EP_DP, None),
        P(EP_DP, None),
        P(EP_DP, None),
        P(EP, None, "dp"),
        P(EP, None, "dp"),
        P(EP, "dp", None),
    )
    out_specs = (P(EP_DP, None), P(EP))
    return jax.shard_map(
        on_device, mesh=finer, in_specs=in_specs, out_specs=out_specs, check_vma=False
    )
```

profile of v0, /device:TPU:0, one launch (start us, length us, event | category | flops | bytes accessed | tf_op | source)
XLA Modules:
  0.0 443.3 jit_solution(7559866327238742268)
XLA Ops:
  7.2 0.0 copy-start
  7.2 0.0 all-gather.2.cloned.1.call-start
  7.2 0.8 copy.22
  8.0 0.1 squeeze_reshape.3
  8.1 0.1 fusion.15
  8.2 0.2 reduce_window_sum.11
  8.4 0.2 fusion.16
  8.6 0.0 copy-done
  8.6 3.2 convolution_convert_fusion.1
  11.8 2.3 copy.24
  14.1 6.7 %all_to_all.27 = bf16[16,2,1,1,8,7168]{5,4,0,3,2,1:T(8,128)(2,1)S(1)} all-to-all(bf16[16,2,1,1,8,7168]{5,4,0,3,2,1:T(8,128)(2,1)S(1)} %copy.24), channel_id=1, replica_groups=mesh['ep_0'=4,'ep_1'=4,'ep_2'=2,'dp'=4] {'ep_2'}, dimensions={1} | all-to-all | bytes 7340032 | tf_op jit(solution)/shard_map/all_to_all | solution.py:28
  20.8 0.3 copy.25
  21.1 53.6 %all_to_all.28 = bf16[16,2,1,1,8,7168]{5,4,1,3,2,0:T(8,128)(2,1)} all-to-all(bf16[16,2,1,1,8,7168]{5,4,1,3,2,0:T(8,128)(2,1)S(1)} %copy.25), channel_id=1, replica_groups=mesh['ep_0'=4,'ep_1'=4,'ep_2'=2,'dp'=4] {'ep_0','ep_1'}, dimensions={0} | all-to-all | bytes 7340032 | tf_op jit(solution)/shard_map/all_to_all | solution.py:28
  74.7 0.0 all-gather.2.cloned.1.call-update
  74.7 0.0 reduce-scatter.2.cloned.1.call-start
  74.7 133.9 %all-gather.2.cloned.1.call-done = bf16[1024,7168]{1,0:T(8,128)(2,1)} async-done(((bf16[256,7168]{1,0:T(8,128)(2,1)}), bf16[1024,7168]{1,0:T(8,128)(2,1)}) %all-gather.2.cloned.1.call-update) | async-done | bytes 14680080 | tf_op jit(solution)/shard_map/all_gather | solution.py:101
  208.6 0.0 copy-start.3
  208.6 0.0 slice-start
  208.7 13.4 %fusion.1 = f32[1024,512]{1,0:T(8,128)S(1)} fusion(bf16[1024,7168]{1,0:T(8,128)(2,1)} %all-gather.2.cloned.1.call-done, bf16[1,7168,512]{2,1,0:T(8,128)(2,1)} %param.10), kind=kOutput, calls=%fused_computation.4 | convolution fusion | flops 7516192768 | bytes 24117248 | tf_op jit(solution)/shard_map/dot_general | solution.py:81
  222.0 0.0 copy-done.3
  222.0 0.0 slice-start.1
  222.0 10.3 %multiply_convert_fusion = bf16[1024,512]{1,0:T(8,128)(2,1)S(1)} fusion(f32[1024,512]{1,0:T(8,128)S(1)} %fusion.1, bf16[1024,7168]{1,0:T(8,128)(2,1)S(1)} %copy-done.3, bf16[1,7168,512]{2,1,0:T(8,128)(2,1)} %param.9), kind=kOutput, calls=%fused_computation.9 | convolution fusion | flops 7519338496 | bytes 25165824 | tf_op jit(solution)/shard_map/dot_general | solution.py:80
  232.3 0.0 slice-done
  232.3 0.0 slice-done.1
  232.3 11.1 %convolution_convert_fusion = bf16[1024,7168]{1,0:T(8,128)(2,1)} fusion(bf16[1024,512]{1,0:T(8,128)(2,1)S(1)} %multiply_convert_fusion, bf16[1,512,7168]{2,1,0:T(8,128)(2,1)S(1)} %bitcast.29), kind=kOutput, calls=%fused_computation | convolution fusion | flops 7523532800 | bytes 23068672 | tf_op jit(solution)/shard_map/dot_general | solution.py:83
  243.4 0.0 reduce-scatter.2.cloned.1.call-update
  243.4 0.0 copy-start.2
  243.4 0.0 copy-start.1
  243.5 0.1 copy.26
  243.5 14.5 %all_to_all.29 = f32[32,1,1]{2,1,0:T(1,128)S(1)} all-to-all(f32[32,1,1]{2,1,0:T(1,128)S(1)} %copy.26), channel_id=1, replica_groups=mesh['ep_0'=4,'ep_1'=4,'ep_2'=2,'dp'=4] {'ep_0','ep_1','ep_2'}, dimensions={0} | all-to-all | bytes 256 | tf_op jit(solution)/shard_map/all_to_all | solution.py:40
  258.1 0.6 reduce_sum.48
  258.7 0.6 broadcast_in_dim.29
  259.4 9.0 %all_to_all.30 = f32[4,1,1]{2,1,0:T(1,128)S(1)} all-to-all(f32[4,1,1]{2,1,0:T(1,128)S(1)} %broadcast_in_dim.29), channel_id=1, replica_groups=mesh['ep_0'=4,'ep_1'=4,'ep_2'=2,'dp'=4] {'dp'}, dimensions={0} | all-to-all | bytes 32 | tf_op jit(solution)/shard_map/all_to_all | solution.py:46
  268.4 107.6 %reduce-scatter.2.cloned.1.call-done = bf16[256,7168]{1,0:T(8,128)(2,1)} async-done(((bf16[1024,7168]{1,0:T(8,128)(2,1)}), bf16[256,7168]{1,0:T(8,128)(2,1)}) %reduce-scatter.2.cloned.1.call-update) | async-done | bytes 3670032 | tf_op jit(solution)/shard_map/reduce_scatter | solution.py:106
  376.0 7.4 %all-to-all-start.2 = ((bf16[32,8,7168]{2,1,0:T(8,128)(2,1)}), bf16[32,8,7168]{2,1,0:T(8,128)(2,1)}, u32[]{:S(2)}, u32[]{:S(2)}) async-start(bf16[32,8,7168]{2,1,0:T(8,128)(2,1)} %bitcast.27), calls=%async_computation.3 | async-start | bytes 7340032 | tf_op jit(solution)/shard_map/all_to_all | solution.py:109
  383.4 0.0 copy-done.2
  383.4 0.1 copy.23
  383.5 0.1 broadcast_in_dim.16
  383.6 0.2 fusion.8
  383.8 0.6 reduce_sum.49
  385.1 45.9 %all-to-all-done.2 = bf16[32,8,7168]{2,1,0:T(8,128)(2,1)} async-done(((bf16[32,8,7168]{2,1,0:T(8,128)(2,1)}), bf16[32,8,7168]{2,1,0:T(8,128)(2,1)}, u32[]{:S(2)}, u32[]{:S(2)}) %all-to-all-start.2) | async-done | bytes 3670048 | tf_op jit(solution)/shard_map/all_to_all | solution.py:109
  431.1 4.3 convolution_convert_fusion.2
  435.3 0.0 copy-done.1
  (6 shorter events, 0.1 us)
Async XLA Ops:
  7.2 1.4 copy-start
  7.2 201.5 %all-gather.2.cloned.1.call-start = ((), (), s32[]{:S(2)}) async-start(), calls=%async_computation.6 | async-start | bytes 18350080 | tf_op jit(solution)/shard_map/all_gather | solution.py:101
  74.7 301.3 %reduce-scatter.2.cloned.1.call-start = ((), (), s32[]{:S(2)}) async-start(), calls=%async_computation.7 | async-start | bytes 18350080 | tf_op jit(solution)/shard_map/reduce_scatter | solution.py:106
  208.6 13.4 %copy-start.3 = (bf16[1024,7168]{1,0:T(8,128)(2,1)S(1)}, bf16[1024,7168]{1,0:T(8,128)(2,1)}, u32[]{:S(2)}) copy-start(bf16[1024,7168]{1,0:T(8,128)(2,1)} %all-gather.2.cloned.1.call-done) | copy-start | bytes 44040196
  208.6 23.7 %slice-start = ((s8[7340032]{0:T(1024)(128)(4,1)}), s8[4194304]{0:T(1024)(128)(4,1)S(1)}, s32[]{:S(2)}) async-start(s8[7340032]{0:T(1024)(128)(4,1)} %bitcast.28), calls=%async_computation.8 | async-start | bytes 8388608
  222.0 10.3 %slice-start.1 = ((s8[7340032]{0:T(1024)(128)(4,1)}), s8[3145728]{0:T(1024)(128)(4,1)S(1)}, s32[]{:S(2)}) async-start(s8[7340032]{0:T(1024)(128)(4,1)} %bitcast.28), calls=%async_computation.9 | async-start | bytes 6291456
  243.4 140.0 %copy-start.2 = (f32[16,8]{0,1:T(8,128)S(1)}, f32[16,8]{0,1:T(8,128)}, u32[]{:S(2)}) copy-start(f32[16,8]{0,1:T(8,128)} %param.8) | copy-start | bytes 1540
  243.4 191.9 %copy-start.1 = (bf16[16,7168]{1,0:T(8,128)(2,1)S(1)}, bf16[16,7168]{1,0:T(8,128)(2,1)}, u32[]{:S(2)}) copy-start(bf16[16,7168]{1,0:T(8,128)(2,1)} %param.6) | copy-start | bytes 688132
  376.0 55.1 %all-to-all-start.2 = ((bf16[32,8,7168]{2,1,0:T(8,128)(2,1)}), bf16[32,8,7168]{2,1,0:T(8,128)(2,1)}, u32[]{:S(2)}, u32[]{:S(2)}) async-start(bf16[32,8,7168]{2,1,0:T(8,128)(2,1)} %bitcast.27), calls=%async_computation.3 | async-start | bytes 7340032 | tf_op jit(solution)/shard_map/all_to_all | solution.py:109
Sparse Core Ops, SparseCore 0:
  74.8 133.7 all-gather.1
  243.5 132.4 reduce-scatter.1
where the time goes:
time: 444 us; the launch traced here: 443 us
  waiting for transfers between devices  288 us (65%)
  blocking collectives  83.8 us (19%)
  matrix products  42.4 us (10%)
  between operations  16 us (4%)
  starting transfers between devices  7.45 us (2%)
    all_gather x1, waiting for transfers between devices, on_device(): lax.all_gather(received.reshape(-1, model_width), 'dp', axis=0, tiled=True)  134 us
    reduce_scatter x1, waiting for transfers between devices, on_device(): lax.psum_scatter(partial_value.astype(jnp.bfloat16), 'dp', scatter_dimens...  108 us
    all_to_all x2, blocking collectives, moved_by_axis(): lax.all_to_all(parts, axes[k], split_axis=k, concat_axis=k, tiled=True)  60.3 us
    all_to_all x1, waiting for transfers between devices, on_device(): lax.all_to_all(shares.reshape(experts, capacity, model_width).astype(jnp....  45.9 us
    all_to_all x1, blocking collectives, sum_at_owner(): parts = lax.all_to_all(split_up(x, dim, devices), axis, 0, 0, tiled=True)  14.5 us
    dot_general x1, matrix products, expert_rows(): up_act = jnp.dot(row_block, up_w, preferred_element_type=jnp.float32)  13.4 us
    dot_general x1, matrix products, expert_rows(): return jnp.dot(hidden, down_w, preferred_element_type=jnp.float32)  11.1 us
    dot_general x1, matrix products, expert_rows(): gate_act = jnp.dot(row_block, gate_w, preferred_element_type=jnp.float32)  10.3 us
  transfers between devices with their start and end apart: 3, of which 3 were waited for; matrix products, arithmetic and copies ran while one was open for 1% of the time, Pallas kernels for 0%

commit v1 on v0

--- a/solution.py
+++ b/solution.py
@@ -98,7 +98,12 @@
     buffer = pack(tokens, own_flat, own_slots, experts, capacity, top_k)
     received = core_and_chips(buffer, (("ep_0", "ep_1"), "ep_2"), (1, 0), 1, 1)
     partial_value = expert_rows(
-        lax.all_gather(received.reshape(-1, model_width), "dp", axis=0, tiled=True),
+        jnp.concatenate(
+            lax.all_to_all(
+                jnp.stack([received.reshape(-1, model_width)] * lax.axis_size("dp")), "dp", 0, 0
+            ),
+            axis=0,
+        ),
         gate_w,
         up_w,
         down_w,

time: 444 us -> 469 us (1.056)
  blocking collectives: 83.8 us -> 243 us
  waiting for transfers between devices: 288 us -> 153 us
    all_to_all x0 -> x1, blocking collectives: none -> 164 us  [on_device(): lax.all_to_all(jnp.stack([received.reshape(-1, model_width)] * lax.axis_s...]
    all_gather x1 -> x0, waiting for transfers between devices: 134 us -> none  [on_device(): lax.all_gather(received.reshape(-1, model_width), 'dp', axis=0, tiled=True)]
    dot_general x1, matrix products: 13.4 us -> 7.71 us  [expert_rows(): up_act = jnp.dot(row_block, up_w, preferred_element_type=jnp.float32)]
  transfers between devices with their start and end apart: 3 -> 2, of which waited for: 3 -> 2; matrix products, arithmetic and copies ran while one was open for 1% -> 1% of each run, Pallas kernels for 0% -> 0%
where the time goes in v1:
time: 469 us; the launch traced here: 468 us
  blocking collectives  243 us (52%)
  waiting for transfers between devices  153 us (33%)
  matrix products  39.7 us (8%)
  between operations  16 us (3%)
  starting transfers between devices  7.43 us (2%)
  local copies, waits for them, and re-layouts  6.33 us (1%)
    all_to_all x1, blocking collectives, on_device(): lax.all_to_all(jnp.stack([received.reshape(-1, model_width)] * lax.axis_s...  164 us
    reduce_scatter x1, waiting for transfers between devices, on_device(): lax.psum_scatter(partial_value.astype(jnp.bfloat16), 'dp', scatter_dimens...  108 us
    all_to_all x2, blocking collectives, moved_by_axis(): lax.all_to_all(parts, axes[k], split_axis=k, concat_axis=k, tiled=True)  60.2 us
    all_to_all x1, waiting for transfers between devices, on_device(): lax.all_to_all(shares.reshape(experts, capacity, model_width).astype(jnp....  45.9 us
    dot_general x1, matrix products, expert_rows(): return jnp.dot(hidden, down_w, preferred_element_type=jnp.float32)  14.1 us
    all_to_all x1, blocking collectives, sum_at_owner(): parts = lax.all_to_all(split_up(x, dim, devices), axis, 0, 0, tiled=True)  11.3 us
    dot_general x1, matrix products, expert_rows(): gate_act = jnp.dot(row_block, gate_w, preferred_element_type=jnp.float32)  10.2 us
  transfers between devices with their start and end apart: 2, of which 2 were waited for; matrix products, arithmetic and copies ran while one was open for 1% of the time, Pallas kernels for 0%

profile of v1, /device:TPU:0, one launch (start us, length us, event | category | flops | bytes accessed | tf_op | source)
XLA Modules:
  0.0 468.1 jit_solution(11718152369794525964)
XLA Ops:
  7.2 0.0 copy-start
  7.2 0.0 reduce-scatter.2.cloned.1.call-start
  7.2 0.8 copy.22
  8.0 0.1 squeeze_reshape.3
  8.1 0.1 fusion.15
  8.2 0.2 reduce_window_sum.11
  8.4 0.2 fusion.16
  8.6 0.0 copy-done
  8.6 3.2 convolution_convert_fusion.1
  11.8 2.3 copy.24
  14.1 6.7 %all_to_all.32 = bf16[16,2,1,1,8,7168]{5,4,0,3,2,1:T(8,128)(2,1)S(1)} all-to-all(bf16[16,2,1,1,8,7168]{5,4,0,3,2,1:T(8,128)(2,1)S(1)} %copy.24), channel_id=1, replica_groups=mesh['ep_0'=4,'ep_1'=4,'ep_2'=2,'dp'=4] {'ep_2'}, dimensions={1} | all-to-all | bytes 7340032 | tf_op jit(solution)/shard_map/all_to_all | solution.py:28
  20.8 0.3 copy.25
  21.1 53.5 %all_to_all.33 = bf16[16,2,1,1,8,7168]{5,4,1,3,2,0:T(8,128)(2,1)S(1)} all-to-all(bf16[16,2,1,1,8,7168]{5,4,1,3,2,0:T(8,128)(2,1)S(1)} %copy.25), channel_id=1, replica_groups=mesh['ep_0'=4,'ep_1'=4,'ep_2'=2,'dp'=4] {'ep_0','ep_1'}, dimensions={0} | all-to-all | bytes 7340032 | tf_op jit(solution)/shard_map/all_to_all | solution.py:28
  74.6 0.0 slice-start
  74.6 1.9 stack.3
  76.5 0.0 slice-start.1
  76.5 164.4 %all_to_all.34 = bf16[4,256,7168]{2,1,0:T(8,128)(2,1)S(1)} all-to-all(bf16[4,256,7168]{2,1,0:T(8,128)(2,1)S(1)} %stack.3), channel_id=1, replica_groups=mesh['ep_0'=4,'ep_1'=4,'ep_2'=2,'dp'=4] {'dp'}, dimensions={0} | all-to-all | bytes 29360128 | tf_op jit(solution)/shard_map/all_to_all | solution.py:102
  240.9 0.0 slice-done
  240.9 0.0 slice-done.1
  240.9 7.7 %fusion.1 = f32[1024,512]{1,0:T(8,128)S(1)} fusion(bf16[1024,7168]{1,0:T(8,128)(2,1)S(1)} %bitcast.26, bf16[1,7168,512]{2,1,0:T(8,128)(2,1)S(1)} %bitcast.32), kind=kOutput, calls=%fused_computation.4 | convolution fusion | flops 7516192768 | bytes 24117248 | tf_op jit(solution)/shard_map/dot_general | solution.py:81
  248.6 10.2 %multiply_convert_fusion = bf16[1024,512]{1,0:T(8,128)(2,1)S(1)} fusion(f32[1024,512]{1,0:T(8,128)S(1)} %fusion.1, bf16[1024,7168]{1,0:T(8,128)(2,1)S(1)} %bitcast.27, bf16[1,7168,512]{2,1,0:T(8,128)(2,1)} %param.9), kind=kOutput, calls=%fused_computation.9 | convolution fusion | flops 7519338496 | bytes 25165824 | tf_op jit(solution)/shard_map/dot_general | solution.py:80
  258.8 14.1 %convolution_convert_fusion = bf16[1024,7168]{1,0:T(8,128)(2,1)} fusion(bf16[1024,512]{1,0:T(8,128)(2,1)S(1)} %multiply_convert_fusion, bf16[1,512,7168]{2,1,0:T(8,128)(2,1)} %param.11), kind=kOutput, calls=%fused_computation | convolution fusion | flops 7523532800 | bytes 23068672 | tf_op jit(solution)/shard_map/dot_general | solution.py:83
  272.9 0.0 reduce-scatter.2.cloned.1.call-update
  272.9 0.0 copy-start.2
  272.9 0.0 copy-start.1
  273.0 0.1 copy.26
  273.0 11.3 %all_to_all.35 = f32[32,1,1]{2,1,0:T(1,128)S(1)} all-to-all(f32[32,1,1]{2,1,0:T(1,128)S(1)} %copy.26), channel_id=1, replica_groups=mesh['ep_0'=4,'ep_1'=4,'ep_2'=2,'dp'=4] {'ep_0','ep_1','ep_2'}, dimensions={0} | all-to-all | bytes 256 | tf_op jit(solution)/shard_map/all_to_all | solution.py:40
  284.3 0.6 reduce_sum.48
  285.0 0.6 broadcast_in_dim.29
  285.6 7.6 %all_to_all.36 = f32[4,1,1]{2,1,0:T(1,128)S(1)} all-to-all(f32[4,1,1]{2,1,0:T(1,128)S(1)} %broadcast_in_dim.29), channel_id=1, replica_groups=mesh['ep_0'=4,'ep_1'=4,'ep_2'=2,'dp'=4] {'dp'}, dimensions={0} | all-to-all | bytes 32 | tf_op jit(solution)/shard_map/all_to_all | solution.py:46
  293.2 107.5 %reduce-scatter.2.cloned.1.call-done = bf16[256,7168]{1,0:T(8,128)(2,1)} async-done(((bf16[1024,7168]{1,0:T(8,128)(2,1)}), bf16[256,7168]{1,0:T(8,128)(2,1)}) %reduce-scatter.2.cloned.1.call-update) | async-done | bytes 3670032 | tf_op jit(solution)/shard_map/reduce_scatter | solution.py:111
  400.8 7.4 %all-to-all-start.3 = ((bf16[32,8,7168]{2,1,0:T(8,128)(2,1)}), bf16[32,8,7168]{2,1,0:T(8,128)(2,1)}, u32[]{:S(2)}, u32[]{:S(2)}) async-start(bf16[32,8,7168]{2,1,0:T(8,128)(2,1)} %bitcast.30), calls=%async_computation.4 | async-start | bytes 7340032 | tf_op jit(solution)/shard_map/all_to_all | solution.py:114
  408.2 0.0 copy-done.2
  408.2 0.1 copy.23
  408.3 0.1 broadcast_in_dim.16
  408.4 0.2 fusion.8
  408.6 0.6 reduce_sum.49
  409.9 45.9 %all-to-all-done.3 = bf16[32,8,7168]{2,1,0:T(8,128)(2,1)} async-done(((bf16[32,8,7168]{2,1,0:T(8,128)(2,1)}), bf16[32,8,7168]{2,1,0:T(8,128)(2,1)}, u32[]{:S(2)}, u32[]{:S(2)}) %all-to-all-start.3) | async-done | bytes 3670048 | tf_op jit(solution)/shard_map/all_to_all | solution.py:114
  455.8 4.3 convolution_convert_fusion.2
  460.1 0.0 copy-done.1
  (6 shorter events, 0.1 us)
Async XLA Ops:
  7.2 1.4 copy-start
  7.2 393.6 %reduce-scatter.2.cloned.1.call-start = ((), (), s32[]{:S(2)}) async-start(), calls=%async_computation.7 | async-start | bytes 18350080 | tf_op jit(solution)/shard_map/reduce_scatter | solution.py:111
  74.6 166.4 %slice-start = ((s8[7340032]{0:T(1024)(128)(4,1)}), s8[4194304]{0:T(1024)(128)(4,1)S(1)}, s32[]{:S(2)}) async-start(s8[7340032]{0:T(1024)(128)(4,1)} %bitcast.31), calls=%async_computation.8 | async-start | bytes 8388608
  76.5 164.4 %slice-start.1 = ((s8[7340032]{0:T(1024)(128)(4,1)}), s8[3145728]{0:T(1024)(128)(4,1)S(1)}, s32[]{:S(2)}) async-start(s8[7340032]{0:T(1024)(128)(4,1)} %bitcast.31), calls=%async_computation.9 | async-start | bytes 6291456
  272.9 135.2 %copy-start.2 = (f32[16,8]{0,1:T(8,128)S(1)}, f32[16,8]{0,1:T(8,128)}, u32[]{:S(2)}) copy-start(f32[16,8]{0,1:T(8,128)} %param.8) | copy-start | bytes 1540
  272.9 187.2 %copy-start.1 = (bf16[16,7168]{1,0:T(8,128)(2,1)S(1)}, bf16[16,7168]{1,0:T(8,128)(2,1)}, u32[]{:S(2)}) copy-start(bf16[16,7168]{1,0:T(8,128)(2,1)} %param.6) | copy-start | bytes 688132
  400.8 55.1 %all-to-all-start.3 = ((bf16[32,8,7168]{2,1,0:T(8,128)(2,1)}), bf16[32,8,7168]{2,1,0:T(8,128)(2,1)}, u32[]{:S(2)}, u32[]{:S(2)}) async-start(bf16[32,8,7168]{2,1,0:T(8,128)(2,1)} %bitcast.30), calls=%async_computation.4 | async-start | bytes 7340032 | tf_op jit(solution)/shard_map/all_to_all | solution.py:114
Sparse Core Ops, SparseCore 0:
  273.0 127.6 reduce-scatter.1
